TPU v7x, 512 devices: a whole 4x4x16 slice. The times are simulated.
512 devices in a mesh: row: 64 (over z_lo, y, x), col: 8 (over z_hi, core).
Axes of the slice: x: 4, y: 4, z: 16 (z_hi: 4, z_lo: 4; z = z_hi * 4 + z_lo), core: 2. Of those that a mesh axis runs over, the one named last changes fastest.
Arguments:
- front: float32 [65536, 1024], P('row', 'col'), may hold values from -6 to 6
- contrib: bfloat16 [524288, 1024], P('row', 'col'), may hold values from -6 to 6
- target: int32 [2048], replicated, may hold values from 0 to 255, as said below
- mask: int32 [256, 8], P('row', 'col'), may hold values 0 or 1
- panel: float32 [65536, 256], P(('row', 'col')), as said below
- pivots: int32 [256], replicated, may hold values from 0 to 65535, as said below
Outputs:
- lower: float32 [65536, 256], P(('row', 'col'))
- schur: float32 [65536, 1024], P('row', 'col')
Inputs may be any that keep to these rules, and one draw needn't show every extreme that they name: Front block row t lies on index t // 4 of row. Within each aligned block of 32 entries (one device's contribution blocks) the values target // 4 are distinct, and index 0 of row receives a block from every aligned block. `pivots`: distinct rows; each aligned group of 1024 rows holds exactly 4 of them. The 256 x 256 matrix formed by the panel's rows named in pivots is invertible.
All inputs are finite; a program needn't handle non-finite values. No bound on the sum of `mask` on one device may be relied on, other than what follows from the above.
Results may differ from a plain program's by a relative error of at most 0.0003.
Values may be sent and summed in bfloat16 or wider, within the bound.
No kernel may reach another device: no remote copies, remote signals or barrier semaphores. Data moves between devices by JAX's collectives and lax.ppermute only.
A program may use at most 64 MiB of HBM per device.

v0:
```python
import jax
import jax.numpy as jnp
from jax import lax
from jax.sharding import PartitionSpec as P

BLK = 256


def exact_dot(left, right):
    return jnp.dot(left, right, precision=lax.Precision.HIGHEST, preferred_element_type=jnp.float32)


def body(front, contrib, target, mask, panel, pivots):
    row_count = lax.axis_size("row")
    col_count = lax.axis_size("col")
    row_index = lax.axis_index("row")
    col_index = lax.axis_index("col")
    tile_rows, tile_cols = front.shape
    blocks_own = tile_rows // BLK
    sent_count = contrib.shape[0] // BLK
    targets = target.reshape(row_count, sent_count)
    own_targets = lax.dynamic_slice_in_dim(targets, row_index, 1, 0)[0]
    device_ids = jnp.arange(row_count, dtype=jnp.int32)
    chooser = (own_targets[None, :] // blocks_own == device_ids[:, None]).astype(jnp.bfloat16)
    pieces = contrib.reshape(sent_count, BLK, tile_cols)
    outgoing = jnp.einsum(
        "db,bxc->dxc", chooser, pieces, preferred_element_type=jnp.float32
    ).astype(jnp.bfloat16)
    arrived = lax.all_to_all(outgoing, "row", split_axis=0, concat_axis=0, tiled=True)
    source_targets = jnp.take(targets, device_ids, axis=0)
    block_ids = jnp.arange(blocks_own, dtype=jnp.int32)
    own_blocks = row_index * blocks_own + block_ids
    placing = jnp.sum(
        (source_targets[:, :, None] == own_blocks[None, None, :]).astype(jnp.float32), axis=1
    ).astype(jnp.bfloat16)
    added = jnp.einsum("sk,sxc->kxc", placing, arrived, preferred_element_type=jnp.float32).reshape(
        tile_rows, tile_cols
    )
    assembled = front + added
    panel_rows = panel.shape[0]
    panel_start = (row_index * col_count + col_index) * panel_rows
    select_rows = (
        pivots[:, None] - panel_start == jnp.arange(panel_rows, dtype=jnp.int32)[None, :]
    ).astype(jnp.float32)
    pivot_block = lax.psum(exact_dot(select_rows, panel), ("row", "col"))
    gram = exact_dot(pivot_block, pivot_block.T)
    factor_low = jnp.linalg.cholesky(gram)
    inverse = jax.scipy.linalg.cho_solve((factor_low, True), pivot_block).T
    local_start = row_index * tile_rows
    picker = (
        pivots[:, None] - local_start == jnp.arange(tile_rows, dtype=jnp.int32)[None, :]
    ).astype(jnp.float32)
    upper = lax.psum(exact_dot(picker, assembled), "row")
    lower_own = exact_dot(panel, inverse)
    update = exact_dot(lax.all_gather(lower_own, "col", axis=0, tiled=True), upper)
    row_mask = jnp.repeat(mask[:, 0].astype(jnp.float32), BLK)
    schur = assembled - row_mask[:, None] * update
    return (lower_own, schur)


def solution(mesh):
    placed = (P("row", "col"), P("row", "col"), P(), P("row", "col"), P(("row", "col"), None), P())
    return jax.shard_map(
        body,
        mesh=mesh,
        in_specs=placed,
        out_specs=(P(("row", "col"), None), P("row", "col")),
        check_vma=False,
    )
```

profile of v0, /device:TPU:2, one launch (start us, length us, event | category | flops | bytes accessed | tf_op | source)
XLA Modules:
  0.0 1228.4 jit_solution(2532103232973570547)
XLA Ops:
  8.0 0.9 reshape.68
  8.9 0.7 copy-done
  9.6 1.8 convolution_convert_fusion
  11.4 4.7 copy.22
  16.1 12.4 %all-to-all-start = ((bf16[64,256,128]{2,1,0:T(8,128)(2,1)}), bf16[64,256,128]{2,1,0:T(8,128)(2,1)}, u32[]{:S(2)}, u32[]{:S(2)}) async-start(bf16[64,256,128]{2,1,0:T(8,128)(2,1)} %copy.22), calls=%async_computation | async-start | bytes 8388608 | tf_op jit(solution)/shard_map/all_to_all | solution.py:29
  28.6 1.0 fusion.12
  29.9 474.1 %all-reduce.4.cloned.1.call-done = f32[256,256]{1,0:T(8,128)} async-done(((f32[256,256]{1,0:T(8,128)}), f32[256,256]{1,0:T(8,128)}) %all-reduce.4.cloned.1.call-update) | async-done | bytes 262160 | tf_op jit(solution)/shard_map/psum | solution.py:45
  504.0 1.5 fusion.30
  505.7 11.7 cholesky.50
  517.5 9.8 custom-call.18
  527.5 0.3 convolution_subtract_fusion.2
  527.7 11.7 cholesky.105
  539.5 0.7 compare_reduce_fusion
  541.6 4.2 while.1
  541.8 0.6 fusion.46
  542.4 1.4 bitcast_dynamic-update-slice_fusion.2
  543.9 0.6 fusion.46
  544.5 1.4 bitcast_dynamic-update-slice_fusion.2
  545.9 0.6 copy-done.6
  546.5 20.5 %custom-call.19 = f32[2,128,128]{1,2,0:T(8,128)S(1)} custom-call(f32[2,128,128]{2,1,0:T(8,128)} %copy-done.6), custom_call_target="InvertDiagBlocksLowerTriangular" | custom-call | tf_op jit(solution)/shard_map/jit(_cho_solve)/triangular_solve | solution.py:48
  567.0 0.3 fusion.10
  567.6 0.3 fusion.19
  568.2 0.3 convolution_subtract_fusion
  568.5 0.3 fusion.17
  568.8 1.0 convolution_bitcast_fusion
  569.9 0.6 gather_fusion
  570.8 4.5 fusion
  575.5 1.3 fusion.4
  576.9 0.8 copy.25
  577.7 41.3 %all-gather.2.cloned.1.call-done = f32[1024,256]{0,1:T(8,128)} async-done(((f32[128,256]{0,1:T(8,128)}), f32[1024,256]{0,1:T(8,128)}) %all-gather.2.cloned.1.call-update) | async-done | bytes 1048592 | tf_op jit(solution)/shard_map/all_gather | solution.py:55
  619.0 598.1 %all-reduce.6.cloned.1.call-done = f32[256,128]{1,0:T(8,128)} async-done(((f32[256,128]{1,0:T(8,128)}), f32[256,128]{1,0:T(8,128)}) %all-reduce.6.cloned.1.call-update) | async-done | bytes 131088 | tf_op jit(solution)/shard_map/psum | solution.py:53
  1217.1 3.9 fusion.3
  (50 shorter events, 2.0 us)
Async XLA Ops:
  8.0 1.6 copy-start
  16.1 12.5 %copy-start.5 = (s32[256]{0:T(256)S(1)}, s32[256]{0:T(256)}, u32[]{:S(2)}) copy-start(s32[256]{0:T(256)} %param.11) | copy-start | bytes 3076
  16.1 12.5 %copy-start.4 = (f32[128,256]{1,0:T(8,128)S(1)}, f32[128,256]{1,0:T(8,128)}, u32[]{:S(2)}) copy-start(f32[128,256]{1,0:T(8,128)} %param.10) | copy-start | bytes 393220
  16.1 554.7 %all-to-all-start = ((bf16[64,256,128]{2,1,0:T(8,128)(2,1)}), bf16[64,256,128]{2,1,0:T(8,128)(2,1)}, u32[]{:S(2)}, u32[]{:S(2)}) async-start(bf16[64,256,128]{2,1,0:T(8,128)(2,1)} %copy.22), calls=%async_computation | async-start | bytes 8388608 | tf_op jit(solution)/shard_map/all_to_all | solution.py:29
  28.5 475.4 %all-reduce.4.cloned.1.call-start = ((), (), s32[]{:S(2)}) async-start(), calls=%async_computation.1 | async-start | bytes 524288 | tf_op jit(solution)/shard_map/psum | solution.py:45
  29.6 541.2 %copy-start.7 = (s32[4,1]{0,1:T(1,128)S(1)}, s32[4,1]{0,1:T(1,128)}, u32[]{:S(2)}) copy-start(s32[4,1]{0,1:T(1,128)} %param.9) | copy-start | bytes 52
  29.7 589.3 %all-gather.2.cloned.1.call-start = ((), (), s32[]{:S(2)}) async-start(), calls=%async_computation.2 | async-start | bytes 1179648 | tf_op jit(solution)/shard_map/all_gather | solution.py:55
  504.0 63.1 %copy-start.1 = (f32[256,256]{1,0:T(8,128)S(1)}, f32[256,256]{1,0:T(8,128)}, u32[]{:S(2)}) copy-start(f32[256,256]{1,0:T(8,128)} %all-reduce.4.cloned.1.call-done) | copy-start | bytes 786436
  545.9 0.7 copy-start.6
  567.6 7.8 copy-start.3
  569.9 647.2 %all-reduce.6.cloned.1.call-start = ((), (), s32[]{:S(2)}) async-start(), calls=%async_computation.3 | async-start | bytes 262144 | tf_op jit(solution)/shard_map/psum | solution.py:53
  570.5 6.4 copy-start.2
Sparse Core Ops, SparseCore 0:
  35.4 468.5 all-reduce.3
  570.0 48.9 all-gather.1
Sparse Core Ops, SparseCore 1:
  576.9 640.1 all-reduce.5
where the time goes:
time: 1230 us
  waiting for transfers between devices  1110 us (90%)
  other arithmetic  54.8 us (4%)
  matrix products  17.3 us (1%)
  between operations  17.1 us (1%)
  local copies, waits for them, and re-layouts  12.7 us (1%)
  starting transfers between devices  12.7 us (1%)
    psum x1, waiting for transfers between devices, body(): upper = lax.psum(exact_dot(picker, assembled), 'row')  598 us
    psum x1, waiting for transfers between devices, body(): pivot_block = lax.psum(exact_dot(select_rows, panel), ('row', 'col'))  474 us
    all_gather x1, waiting for transfers between devices, body(): lax.all_gather(lower_own, 'col', axis=0, tiled=True)  41.3 us
    another operation x6, other arithmetic, body(): factor_low = jnp.linalg.cholesky(gram)  34 us
  transfers between devices with their start and end apart: 4, of which 3 were waited for; matrix products, arithmetic and copies ran while one was open for 6% of the time, Pallas kernels for 0%

commit v1 on v0

--- a/solution.py
+++ b/solution.py
@@ -42,7 +42,7 @@
     select_rows = (
         pivots[:, None] - panel_start == jnp.arange(panel_rows, dtype=jnp.int32)[None, :]
     ).astype(jnp.float32)
-    pivot_block = lax.psum(exact_dot(select_rows, panel), ("row", "col"))
+    pivot_block = lax.psum(lax.psum(exact_dot(select_rows, panel), "col"), "row")
     gram = exact_dot(pivot_block, pivot_block.T)
     factor_low = jnp.linalg.cholesky(gram)
     inverse = jax.scipy.linalg.cho_solve((factor_low, True), pivot_block).T

time: 1230 us -> 966 us (0.79)
  the two profiles are of different devices: /device:TPU:2 before, /device:TPU:97 now
where the time goes in v1:
time: 966 us
  waiting for transfers between devices  851 us (88%)
  other arithmetic  54.8 us (6%)
  matrix products  19 us (2%)
  between operations  15.3 us (2%)
  local copies, waits for them, and re-layouts  14.8 us (2%)
  starting transfers between devices  11 us (1%)
    psum x1, waiting for transfers between devices, body(): lax.psum(lax.psum(exact_dot(select_rows, panel), 'col'), 'row')  630 us
    all_gather x1, waiting for transfers between devices, body(): lax.all_gather(lower_own, 'col', axis=0, tiled=True)  115 us
    all_to_all x1, waiting for transfers between devices, body(): lax.all_to_all(outgoing, 'row', split_axis=0, concat_axis=0, tiled=True)  96.8 us
    another operation x6, other arithmetic, body(): factor_low = jnp.linalg.cholesky(gram)  33.9 us
    another operation x3, other arithmetic, body(): inverse = jax.scipy.linalg.cho_solve((factor_low, True), pivot_block).T  20.5 us
  transfers between devices with their start and end apart: 4, of which 4 were waited for; matrix products, arithmetic and copies ran while one was open for 1% of the time, Pallas kernels for 0%

profile of v1, /device:TPU:97, one launch (start us, length us, event | category | flops | bytes accessed | tf_op | source)
XLA Modules:
  0.0 965.9 jit_solution(14206416541938358378)
XLA Ops:
  7.2 0.9 reshape.68
  8.1 0.7 copy-done
  8.8 1.8 convolution_convert_fusion
  10.6 4.7 copy.22
  15.3 10.7 %all-to-all-start = ((bf16[64,256,128]{2,1,0:T(8,128)(2,1)}), bf16[64,256,128]{2,1,0:T(8,128)(2,1)}, u32[]{:S(2)}, u32[]{:S(2)}) async-start(bf16[64,256,128]{2,1,0:T(8,128)(2,1)} %copy.22), calls=%async_computation | async-start | bytes 8388608 | tf_op jit(solution)/shard_map/all_to_all | solution.py:29
  26.1 1.0 fusion.12
  27.2 0.6 gather_fusion
  28.1 96.8 %all-to-all-done = bf16[64,256,128]{2,1,0:T(8,128)(2,1)} async-done(((bf16[64,256,128]{2,1,0:T(8,128)(2,1)}), bf16[64,256,128]{2,1,0:T(8,128)(2,1)}, u32[]{:S(2)}, u32[]{:S(2)}) %all-to-all-start) | async-done | bytes 4194336 | tf_op jit(solution)/shard_map/all_to_all | solution.py:29
  124.9 4.5 fusion
  129.5 1.3 fusion.4
  130.9 8.4 all-reduce.5.cloned.1.call-done
  139.5 630.5 %all-reduce.7.cloned.1.call-done = (f32[256,256]{1,0:T(8,128)}, f32[256,128]{1,0:T(8,128)}) async-done(((f32[256,256]{1,0:T(8,128)}, f32[256,128]{1,0:T(8,128)}), (f32[256,256]{1,0:T(8,128)}, f32[256,128]{1,0:T(8,128)})) %all-reduce.7.cloned.1.call-update) | async-done | bytes 393232 | tf_op jit(solution)/shard_map/psum | solution.py:45
  770.0 1.5 fusion.30
  771.7 0.7 copy-done.2
  772.4 11.7 %cholesky.50 = f32[128,128]{1,0:T(8,128)S(1)} custom-call(f32[128,128]{1,0:T(8,128)S(1)} %cholesky.118), custom_call_target="Cholesky" | custom-call | tf_op jit(solution)/shard_map/jit(cholesky)/cholesky | solution.py:47
  784.2 9.8 %custom-call.18 = f32[1,128,128]{1,2,0:T(8,128)S(1)} custom-call(f32[1,128,128]{2,1,0:T(8,128)S(1)} %get-tuple-element.33), custom_call_target="InvertDiagBlocksLowerTriangular" | custom-call | tf_op jit(solution)/shard_map/jit(cholesky)/cholesky | solution.py:47
  794.0 1.0 constant_dynamic-update-slice_fusion
  795.1 1.1 convolution_subtract_fusion.2
  796.2 11.7 %cholesky.105 = f32[128,128]{1,0:T(8,128)S(1)} custom-call(f32[128,128]{1,0:T(8,128)S(1)} %convolution_subtract_fusion.2), custom_call_target="Cholesky" | custom-call | tf_op jit(solution)/shard_map/jit(cholesky)/cholesky | solution.py:47
  807.9 0.6 compare_reduce_fusion
  810.0 5.4 while.1
  810.2 0.6 fusion.46
  810.7 2.0 bitcast_dynamic-update-slice_fusion.2
  812.8 0.6 fusion.46
  813.3 2.0 bitcast_dynamic-update-slice_fusion.2
  815.4 20.5 %custom-call.19 = f32[2,128,128]{1,2,0:T(8,128)S(1)} custom-call(f32[2,128,128]{2,1,0:T(8,128)} %get-tuple-element.9), custom_call_target="InvertDiagBlocksLowerTriangular" | custom-call | tf_op jit(solution)/shard_map/jit(_cho_solve)/triangular_solve | solution.py:48
  836.4 0.3 fusion.19
  837.0 0.3 convolution_subtract_fusion
  837.6 1.0 convolution_bitcast_fusion
  838.8 1.7 copy.25
  840.4 115.1 %all-gather.2.cloned.1.call-done = f32[1024,256]{0,1:T(8,128)} async-done(((f32[128,256]{0,1:T(8,128)}), f32[1024,256]{0,1:T(8,128)}) %all-gather.2.cloned.1.call-update) | async-done | bytes 1048592 | tf_op jit(solution)/shard_map/all_gather | solution.py:55
  955.5 3.9 fusion.3
  (48 shorter events, 2.3 us)
Async XLA Ops:
  7.2 1.6 copy-start
  15.3 10.8 %copy-start.5 = (s32[256]{0:T(256)S(1)}, s32[256]{0:T(256)}, u32[]{:S(2)}) copy-start(s32[256]{0:T(256)} %param.11) | copy-start | bytes 3076
  15.3 10.8 %copy-start.4 = (f32[128,256]{1,0:T(8,128)S(1)}, f32[128,256]{1,0:T(8,128)}, u32[]{:S(2)}) copy-start(f32[128,256]{1,0:T(8,128)} %param.10) | copy-start | bytes 393220
  15.3 109.6 %all-to-all-start = ((bf16[64,256,128]{2,1,0:T(8,128)(2,1)}), bf16[64,256,128]{2,1,0:T(8,128)(2,1)}, u32[]{:S(2)}, u32[]{:S(2)}) async-start(bf16[64,256,128]{2,1,0:T(8,128)(2,1)} %copy.22), calls=%async_computation | async-start | bytes 8388608 | tf_op jit(solution)/shard_map/all_to_all | solution.py:29
  26.0 103.4 %copy-start.3 = (f32[1024,128]{1,0:T(8,128)S(1)}, f32[1024,128]{1,0:T(8,128)}, u32[]{:S(2)}) copy-start(f32[1024,128]{1,0:T(8,128)} %param.6) | copy-start | bytes 1572868
  26.0 113.2 %all-reduce.5.cloned.1.call-start = ((), (), s32[]{:S(2)}) async-start(), calls=%async_computation.1 | async-start | bytes 524288 | tf_op jit(solution)/shard_map/psum | solution.py:45
  27.1 742.9 %all-reduce.7.cloned.1.call-start = ((), (), s32[]{:S(2)}) async-start(), calls=%async_computation.3 | async-start | bytes 786432 | tf_op jit(solution)/shard_map/psum | solution.py:45
  129.5 709.2 %copy-start.6 = (s32[4,1]{0,1:T(1,128)S(1)}, s32[4,1]{0,1:T(1,128)}, u32[]{:S(2)}) copy-start(s32[4,1]{0,1:T(1,128)} %param.9) | copy-start | bytes 52
  139.3 816.2 %all-gather.2.cloned.1.call-start = ((), (), s32[]{:S(2)}) async-start(), calls=%async_computation.2 | async-start | bytes 1179648 | tf_op jit(solution)/shard_map/all_gather | solution.py:55
  770.0 65.8 %copy-start.1 = (f32[256,256]{1,0:T(8,128)S(1)}, f32[256,256]{1,0:T(8,128)}, u32[]{:S(2)}) copy-start(f32[256,256]{1,0:T(8,128)} %get-tuple-element.26) | copy-start | bytes 786436
  771.7 0.7 copy-start.2
Sparse Core Ops, SparseCore 0:
  30.3 108.8 all-reduce.4
  143.1 626.8 all-reduce.6
  838.8 116.6 all-gather.1

commit v2 on v0

--- a/solution.py
+++ b/solution.py
@@ -50,7 +50,7 @@
     picker = (
         pivots[:, None] - local_start == jnp.arange(tile_rows, dtype=jnp.int32)[None, :]
     ).astype(jnp.float32)
-    upper = lax.psum(exact_dot(picker, assembled), "row")
+    upper = jnp.sum(lax.all_gather(exact_dot(picker, assembled), "row"), axis=0)
     lower_own = exact_dot(panel, inverse)
     update = exact_dot(lax.all_gather(lower_own, "col", axis=0, tiled=True), upper)
     row_mask = jnp.repeat(mask[:, 0].astype(jnp.float32), BLK)

time: 1230 us -> 639 us (0.52)
  the two profiles are of different devices: /device:TPU:2 before, /device:TPU:97 now
where the time goes in v2:
time: 639 us; the launch traced here: 638 us
  waiting for transfers between devices  518 us (81%)
  other arithmetic  58.6 us (9%)
  matrix products  19 us (3%)
  between operations  17.1 us (3%)
  local copies, waits for them, and re-layouts  14.9 us (2%)
  starting transfers between devices  11 us (2%)
    psum x1, waiting for transfers between devices, body(): pivot_block = lax.psum(exact_dot(select_rows, panel), ('row', 'col'))  377 us
    all_to_all x1, waiting for transfers between devices, body(): lax.all_to_all(outgoing, 'row', split_axis=0, concat_axis=0, tiled=True)  90.4 us
    all_gather x1, waiting for transfers between devices, body(): lax.all_gather(lower_own, 'col', axis=0, tiled=True)  50.1 us
    another operation x6, other arithmetic, body(): factor_low = jnp.linalg.cholesky(gram)  34 us
    another operation x3, other arithmetic, body(): inverse = jax.scipy.linalg.cho_solve((factor_low, True), pivot_block).T  20.5 us
  transfers between devices with their start and end apart: 4, of which 3 were waited for; matrix products, arithmetic and copies ran while one was open for 13% of the time, Pallas kernels for 0%

profile of v2, /device:TPU:97, one launch (start us, length us, event | category | flops | bytes accessed | tf_op | source)
XLA Modules:
  0.0 638.5 jit_solution(16175735417411919406)
XLA Ops:
  8.0 0.9 reshape.68
  8.9 0.7 copy-done
  9.6 1.8 convolution_convert_fusion
  11.4 4.7 copy.22
  16.1 10.7 %all-to-all-start = ((bf16[64,256,128]{2,1,0:T(8,128)(2,1)}), bf16[64,256,128]{2,1,0:T(8,128)(2,1)}, u32[]{:S(2)}, u32[]{:S(2)}) async-start(bf16[64,256,128]{2,1,0:T(8,128)(2,1)} %copy.22), calls=%async_computation | async-start | bytes 8388608 | tf_op jit(solution)/shard_map/all_to_all | solution.py:29
  26.9 1.0 fusion.12
  28.0 0.6 gather_fusion
  28.9 90.4 %all-to-all-done = bf16[64,256,128]{2,1,0:T(8,128)(2,1)} async-done(((bf16[64,256,128]{2,1,0:T(8,128)(2,1)}), bf16[64,256,128]{2,1,0:T(8,128)(2,1)}, u32[]{:S(2)}, u32[]{:S(2)}) %all-to-all-start) | async-done | bytes 4194336 | tf_op jit(solution)/shard_map/all_to_all | solution.py:29
  119.3 4.6 fusion
  123.9 1.3 fusion.4
  125.6 377.1 %all-reduce.3.cloned.1.call-done = f32[256,256]{1,0:T(8,128)} async-done(((f32[256,256]{1,0:T(8,128)}), f32[256,256]{1,0:T(8,128)}) %all-reduce.3.cloned.1.call-update) | async-done | bytes 262160 | tf_op jit(solution)/shard_map/psum | solution.py:45
  502.6 1.5 fusion.30
  504.4 0.7 copy-done.2
  505.1 11.7 %cholesky.50 = f32[128,128]{1,0:T(8,128)S(1)} custom-call(f32[128,128]{1,0:T(8,128)S(1)} %cholesky.118), custom_call_target="Cholesky" | custom-call | tf_op jit(solution)/shard_map/jit(cholesky)/cholesky | solution.py:47
  516.8 9.8 %custom-call.18 = f32[1,128,128]{1,2,0:T(8,128)S(1)} custom-call(f32[1,128,128]{2,1,0:T(8,128)S(1)} %get-tuple-element.31), custom_call_target="InvertDiagBlocksLowerTriangular" | custom-call | tf_op jit(solution)/shard_map/jit(cholesky)/cholesky | solution.py:47
  526.6 1.0 constant_dynamic-update-slice_fusion
  527.7 1.1 convolution_subtract_fusion.2
  528.8 11.7 %cholesky.105 = f32[128,128]{1,0:T(8,128)S(1)} custom-call(f32[128,128]{1,0:T(8,128)S(1)} %convolution_subtract_fusion.2), custom_call_target="Cholesky" | custom-call | tf_op jit(solution)/shard_map/jit(cholesky)/cholesky | solution.py:47
  540.6 0.7 compare_reduce_fusion
  542.7 5.5 while.1
  542.9 0.6 fusion.46
  543.5 2.0 bitcast_dynamic-update-slice_fusion.2
  545.5 0.6 fusion.46
  546.1 2.0 bitcast_dynamic-update-slice_fusion.2
  548.2 20.5 %custom-call.19 = f32[2,128,128]{1,2,0:T(8,128)S(1)} custom-call(f32[2,128,128]{2,1,0:T(8,128)} %get-tuple-element.9), custom_call_target="InvertDiagBlocksLowerTriangular" | custom-call | tf_op jit(solution)/shard_map/jit(_cho_solve)/triangular_solve | solution.py:48
  569.3 0.3 fusion.19
  569.8 0.3 convolution_subtract_fusion
  570.4 1.0 convolution_bitcast_fusion
  571.6 1.7 copy.25
  573.3 3.8 reduce_sum.19
  577.0 50.1 %all-gather.4.cloned.1.call-done = f32[1024,256]{0,1:T(8,128)} async-done(((f32[128,256]{0,1:T(8,128)}), f32[1024,256]{0,1:T(8,128)}) %all-gather.4.cloned.1.call-update) | async-done | bytes 1048592 | tf_op jit(solution)/shard_map/all_gather | solution.py:55
  627.2 3.9 fusion.3
  (49 shorter events, 2.3 us)
Async XLA Ops:
  8.0 1.6 copy-start
  16.1 10.8 %copy-start.5 = (s32[256]{0:T(256)S(1)}, s32[256]{0:T(256)}, u32[]{:S(2)}) copy-start(s32[256]{0:T(256)} %param.11) | copy-start | bytes 3076
  16.1 10.8 %copy-start.4 = (f32[128,256]{1,0:T(8,128)S(1)}, f32[128,256]{1,0:T(8,128)}, u32[]{:S(2)}) copy-start(f32[128,256]{1,0:T(8,128)} %param.10) | copy-start | bytes 393220
  16.1 103.2 %all-to-all-start = ((bf16[64,256,128]{2,1,0:T(8,128)(2,1)}), bf16[64,256,128]{2,1,0:T(8,128)(2,1)}, u32[]{:S(2)}, u32[]{:S(2)}) async-start(bf16[64,256,128]{2,1,0:T(8,128)(2,1)} %copy.22), calls=%async_computation | async-start | bytes 8388608 | tf_op jit(solution)/shard_map/all_to_all | solution.py:29
  26.8 97.0 %copy-start.3 = (f32[1024,128]{1,0:T(8,128)S(1)}, f32[1024,128]{1,0:T(8,128)}, u32[]{:S(2)}) copy-start(f32[1024,128]{1,0:T(8,128)} %param.6) | copy-start | bytes 1572868
  26.8 475.8 %all-reduce.3.cloned.1.call-start = ((), (), s32[]{:S(2)}) async-start(), calls=%async_computation.1 | async-start | bytes 524288 | tf_op jit(solution)/shard_map/psum | solution.py:45
  28.0 545.3 %all-gather.6.cloned.1.call-start = ((), (), s32[]{:S(2)}) async-start(), calls=%async_computation.3 | async-start | bytes 8519680 | tf_op jit(solution)/shard_map/all_gather | solution.py:53
  123.9 447.6 %copy-start.6 = (s32[4,1]{0,1:T(1,128)S(1)}, s32[4,1]{0,1:T(1,128)}, u32[]{:S(2)}) copy-start(s32[4,1]{0,1:T(1,128)} %param.9) | copy-start | bytes 52
  125.3 501.9 %all-gather.4.cloned.1.call-start = ((), (), s32[]{:S(2)}) async-start(), calls=%async_computation.2 | async-start | bytes 1179648 | tf_op jit(solution)/shard_map/all_gather | solution.py:55
  502.6 66.0 %copy-start.1 = (f32[256,256]{1,0:T(8,128)S(1)}, f32[256,256]{1,0:T(8,128)}, u32[]{:S(2)}) copy-start(f32[256,256]{1,0:T(8,128)} %all-reduce.3.cloned.1.call-done) | copy-start | bytes 786436
  504.3 0.7 copy-start.2
Sparse Core Ops, SparseCore 0:
  33.7 468.9 all-reduce.2
Sparse Core Ops, SparseCore 1:
  125.4 294.7 all-gather.5
  571.6 55.5 all-gather.3
